TPU v7x, 512 devices: a whole 4x8x8 slice. The times are simulated.
512 devices in a mesh: fix: 64 (over z, x, core), subj: 8 (over y).
Axes of the slice: x: 4, y: 8, z: 8, core: 2. Of those that a mesh axis runs over, the one named last changes fastest.
Arguments:
- fixels: float32 [65536, 1024], P('fix', 'subj'), may hold values from -6 to 6
- conn_tiles: float32 [512, 4, 128, 128], P('fix'), may hold values from -0.25 to 0.25
- columns: int32 [512, 4], P('fix'), may hold values from 0 to 511, as said below
- nuisance: float32 [4, 1024], P(None, 'subj'), may hold values from -5 to 5
- nuisance_pinv: float32 [4, 1024], P(None, 'subj'), may hold values from -0.1875 to 0.1875
- contrast: float32 [4, 1024], replicated, may hold values from -0.1875 to 0.1875
- perm_table: int32 [128, 1024], P(None, 'subj'), may hold values from 0 to 1023, each once within a row
Outputs:
- projections: float32 [512, 65536], P('subj', 'fix')
Inputs may be any that keep to these rules, and one draw needn't show every extreme that they name: `columns`: device j of fix holds blocks j * 8 to (j + 1) * 8 - 1. The 32 entries of one device's rows name blocks of any one device at most 1 times, and in every draw some device's blocks are named exactly 1 times by the rows of every device. `perm_table`: each row is a permutation of the 1024 subjects.
All inputs are finite; a program needn't handle non-finite values.
Results may differ from a plain program's by a relative error of at most 0.000071.
Values sent between devices are 32-bit elements; how exact they have to be, the bound alone decides.
A program may use at most 64 MiB of HBM per device.

v0:
```python
import jax
import jax.numpy as jnp
from jax import lax
from jax.sharding import PartitionSpec as P


def design_rows(contrast, perm_table):
    picked = jnp.take(contrast, perm_table, axis=1)
    return jnp.transpose(picked, (1, 0, 2)).reshape(-1, perm_table.shape[1])


def per_device(fixels, conn_tiles, columns, nuisance, nuisance_pinv, contrast, perm_table):
    fix_count = lax.axis_size("fix")
    block_count, per_row = columns.shape
    block_size = conn_tiles.shape[2]
    subj_count = fixels.shape[1]
    tile_total = block_count * per_row
    wanted = columns.reshape(tile_total)
    owners = wanted // block_count
    local_index = wanted % block_count
    capacity = (tile_total + fix_count - 1) // fix_count
    positions = jnp.arange(tile_total)
    earlier = positions[:, None] > positions[None, :]
    same_owner = owners[:, None] == owners[None, :]
    ranks = jnp.sum(jnp.logical_and(same_owner, earlier), axis=1)
    slots = owners * capacity + ranks
    request = jnp.zeros((fix_count * capacity,), jnp.int32).at[slots].set(local_index)
    asked = lax.all_to_all(
        request.reshape(fix_count, capacity), "fix", split_axis=0, concat_axis=0, tiled=True
    ).reshape(-1)
    design = design_rows(contrast, perm_table)
    own_blocks = fixels.reshape(block_count, block_size, subj_count)
    outgoing = jnp.take(own_blocks, asked, axis=0).reshape(
        fix_count, capacity, block_size, subj_count
    )
    arrived = lax.all_to_all(outgoing, "fix", split_axis=0, concat_axis=0, tiled=True).reshape(
        fix_count * capacity, block_size, subj_count
    )
    needed = jnp.take(arrived, slots, axis=0).reshape(block_count, per_row, block_size, subj_count)
    smoothed = jnp.einsum(
        "bkij,bkjs->bis", conn_tiles, needed, precision=lax.Precision.HIGHEST
    ).reshape(block_count * block_size, subj_count)
    fitted_part = jnp.einsum("ns,fs->nf", nuisance_pinv, smoothed, precision=lax.Precision.HIGHEST)
    fitted = lax.psum(fitted_part, "subj")
    residual = smoothed - jnp.einsum("nf,ns->fs", fitted, nuisance, precision=lax.Precision.HIGHEST)
    partial_value = jnp.einsum("cs,fs->cf", design, residual, precision=lax.Precision.HIGHEST)
    return lax.psum_scatter(partial_value, "subj", scatter_dimension=0, tiled=True)


def solution(mesh):
    placed = (
        P("fix", "subj"),
        P("fix", None, None, None),
        P("fix", None),
        P(None, "subj"),
        P(None, "subj"),
        P(),
        P(None, "subj"),
    )
    return jax.shard_map(
        per_device, mesh=mesh, in_specs=placed, out_specs=P("subj", "fix"), check_vma=False
    )
```

profile of v0, /device:TPU:6, one launch (start us, length us, event | category | flops | bytes accessed | tf_op | source)
XLA Modules:
  0.0 232.2 jit_solution(1409098919103364654)
XLA Ops:
  6.5 0.0 copy-start
  6.5 0.9 copy.43
  7.4 0.1 reshape.202
  7.5 0.1 reshape.203
  7.6 0.2 convert_reduce_fusion
  7.8 0.7 scatter_custom_fusion
  8.5 0.1 copy.49
  8.6 21.5 %all_to_all.20 = s32[64,1,1]{2,1,0:T(1,128)S(1)} all-to-all(s32[64,1,1]{2,1,0:T(1,128)S(1)} %copy.49), channel_id=1, replica_groups=mesh['fix'=64,'subj'=8] {'fix'}, dimensions={0} | all-to-all | bytes 512 | tf_op jit(solution)/shard_map/all_to_all | solution.py:28
  30.1 1.2 reduce
  31.4 3.8 %gather_fusion.1 = f32[64,128,128]{2,1,0:T(8,128)} fusion(f32[8,128,128]{2,1,0:T(8,128)} %bitcast.37, s32[1024]{0:T(1024)S(1)} %pad_clamp_fusion.1), kind=kCustom, calls=%fused_computation.1 | custom fusion | bytes 8388864 | tf_op jit(solution)/shard_map/jit(_take)/gather | solution.py:33
  35.2 4.5 %bitcast_select_fusion = f32[64,1,128,128]{3,2,1,0:T(8,128)} fusion(f32[64,128,128]{2,1,0:T(8,128)} %gather_fusion.1, pred[64]{0:T(512)(128)(4,1)S(1)} %compare_and_fusion.2), kind=kLoop, calls=%fused_computation.4 | loop fusion | flops 1048576 | bytes 8388672 | tf_op jit(solution)/shard_map/jit(_take)/select_n | solution.py:33
  39.7 7.4 %all-to-all-start.1 = ((f32[64,1,128,128]{3,2,1,0:T(8,128)}), f32[64,1,128,128]{3,2,1,0:T(8,128)}, u32[]{:S(2)}, u32[]{:S(2)}) async-start(f32[64,1,128,128]{3,2,1,0:T(8,128)} %bitcast_select_fusion), calls=%async_computation.1 | async-start | bytes 8388608 | tf_op jit(solution)/shard_map/all_to_all | solution.py:36
  47.1 0.0 reduce-scatter.2.cloned.1.call-start
  47.1 0.1 reduce_sum.14
  47.2 0.0 copy-done.2
  47.2 0.2 copy.41
  47.4 0.0 copy-done.1
  47.5 54.4 %gather_fusion = f32[16384,4]{1,0:T(8,128)} fusion(f32[4,1024]{0,1:T(8,128)S(1)} %copy.41, s32[16384]{0:T(1024)S(1)} %bitcast_clamp_fusion), kind=kCustom, calls=%fused_computation | custom fusion | bytes 589824 | tf_op jit(solution)/shard_map/jit(_take)/gather | solution.py:8
  101.9 5.5 %copy.42 = f32[128,128,4]{1,2,0:T(4,128)S(1)} copy(f32[128,128,4]{2,1,0:T(8,128)} %bitcast.38) | data formatting | bytes 524288 | tf_op jit(solution)/shard_map/jit(_take)/gather | solution.py:8
  107.4 0.1 broadcast_select_fusion
  107.5 35.7 %all-to-all-done.1 = f32[64,1,128,128]{3,2,1,0:T(8,128)} async-done(((f32[64,1,128,128]{3,2,1,0:T(8,128)}), f32[64,1,128,128]{3,2,1,0:T(8,128)}, u32[]{:S(2)}, u32[]{:S(2)}) %all-to-all-start.1) | async-done | bytes 4194336 | tf_op jit(solution)/shard_map/all_to_all | solution.py:36
  143.3 4.2 %gather_fusion.2 = f32[32,128,128]{2,1,0:T(8,128)} fusion(f32[64,128,128]{2,1,0:T(8,128)} %bitcast.10, s32[1024]{0:T(1024)S(1)} %pad_clamp_fusion), kind=kCustom, calls=%fused_computation.2 | custom fusion | bytes 4194432 | tf_op jit(solution)/shard_map/jit(_take)/gather | solution.py:39
  147.5 0.0 copy-done
  147.5 4.1 %fusion = f32[8,128,128,1]{1,2,3,0:T(8,128)S(1)} fusion(f32[8,4,128,128]{3,2,1,0:T(8,128)S(1)} %copy-done, f32[8,4,128,128]{3,2,1,0:T(8,128)} %bitcast.39, pred[8,4]{1,0:T(8,128)(4,1)S(1)} %compare_and_fusion.1), kind=kOutput, calls=%fused_computation.5 | convolution fusion | flops 805830656 | bytes 4718624 | tf_op jit(solution)/shard_map/bkij,bkjs->bis/dot_general | solution.py:40
  151.6 0.0 copy-done.3
  151.6 0.5 convolution_bitcast_fusion
  152.2 30.4 %psum.7 = f32[4,1024]{1,0:T(4,128)S(1)} all-reduce(f32[4,1024]{1,0:T(4,128)S(1)} %convolution_bitcast_fusion), channel_id=1, replica_groups=mesh['fix'=64,'subj'=8] {'subj'}, use_global_device_ids=true, to_apply=%region_2.3 | all-reduce | flops 4096 | bytes 32768 | tf_op jit(solution)/shard_map/psum | solution.py:44
  182.5 0.0 copy-done.4
  182.5 1.0 convolution_subtract_fusion
  183.5 3.2 %fusion.13 = f32[512,1024]{1,0:T(8,128)} fusion(f32[512,128]{1,0:T(8,128)S(1)} %bitcast.42, f32[1024,128]{1,0:T(8,128)S(1)} %convolution_subtract_fusion), kind=kOutput, calls=%fused_computation.49 | convolution fusion | flops 805306368 | bytes 2883584 | tf_op jit(solution)/shard_map/cs,fs->cf/dot_general | solution.py:46
  186.7 0.0 reduce-scatter.2.cloned.1.call-update
  186.7 38.6 %reduce-scatter.2.cloned.1.call-done = f32[64,1024]{1,0:T(8,128)} async-done(((f32[512,1024]{1,0:T(8,128)}), f32[64,1024]{1,0:T(8,128)}) %reduce-scatter.2.cloned.1.call-update) | async-done | bytes 262160 | tf_op jit(solution)/shard_map/reduce_scatter | solution.py:47
  (13 shorter events, 0.1 us)
Async XLA Ops:
  6.5 140.9 %copy-start = (f32[8,4,128,128]{3,2,1,0:T(8,128)S(1)}, f32[8,4,128,128]{3,2,1,0:T(8,128)}, u32[]{:S(2)}) copy-start(f32[8,4,128,128]{3,2,1,0:T(8,128)} %param.8) | copy-start | bytes 6291460
  39.7 7.5 %copy-start.2 = (f32[4,1024]{1,0:T(4,128)S(1)}, f32[4,1024]{1,0:T(4,128)}, u32[]{:S(2)}) copy-start(f32[4,1024]{1,0:T(4,128)} %param.12) | copy-start | bytes 49156
  39.7 7.7 %copy-start.1 = (s32[128,128]{1,0:T(8,128)S(1)}, s32[128,128]{1,0:T(8,128)}, u32[]{:S(2)}) copy-start(s32[128,128]{1,0:T(8,128)} %param.13) | copy-start | bytes 196612
  39.7 103.6 %all-to-all-start.1 = ((f32[64,1,128,128]{3,2,1,0:T(8,128)}), f32[64,1,128,128]{3,2,1,0:T(8,128)}, u32[]{:S(2)}, u32[]{:S(2)}) async-start(f32[64,1,128,128]{3,2,1,0:T(8,128)} %bitcast_select_fusion), calls=%async_computation.1 | async-start | bytes 8388608 | tf_op jit(solution)/shard_map/all_to_all | solution.py:36
  47.1 178.3 %reduce-scatter.2.cloned.1.call-start = ((), (), s32[]{:S(2)}) async-start(), calls=%async_computation.3 | async-start | bytes 2359296 | tf_op jit(solution)/shard_map/reduce_scatter | solution.py:47
  147.5 4.1 %copy-start.3 = (f32[4,128]{1,0:T(4,128)S(1)}, f32[4,128]{1,0:T(4,128)}, u32[]{:S(2)}) copy-start(f32[4,128]{1,0:T(4,128)} %param.11) | copy-start | bytes 6148
  147.5 35.1 %copy-start.4 = (f32[4,128]{1,0:T(4,128)S(1)}, f32[4,128]{1,0:T(4,128)}, u32[]{:S(2)}) copy-start(f32[4,128]{1,0:T(4,128)} %param.10) | copy-start | bytes 6148
Sparse Core Ops, SparseCore 0:
  186.8 38.4 reduce-scatter.1
where the time goes:
time: 233 us; the launch traced here: 232 us
  waiting for transfers between devices  74.4 us (32%)
  local copies, waits for them, and re-layouts  70.1 us (30%)
  blocking collectives  51.9 us (22%)
  between operations  13.5 us (6%)
  matrix products  8.82 us (4%)
  starting transfers between devices  7.41 us (3%)
  other arithmetic  6.09 us (3%)
    gather x2, local copies, waits for them, and re-layouts, design_rows(): picked = jnp.take(contrast, perm_table, axis=1)  59.9 us
    reduce_scatter x1, waiting for transfers between devices, per_device(): lax.psum_scatter(partial_value, 'subj', scatter_dimension=0, tiled=True)  38.6 us
    all_to_all x1, waiting for transfers between devices, per_device(): lax.all_to_all(outgoing, 'fix', split_axis=0, concat_axis=0, tiled=True)  35.7 us
    psum x1, blocking collectives, per_device(): fitted = lax.psum(fitted_part, 'subj')  30.4 us
    all_to_all x1, blocking collectives, per_device(): lax.all_to_all(request.reshape(fix_count, capacity), 'fix', split_axis=0,...  21.5 us
    all_to_all x1, starting transfers between devices, per_device(): lax.all_to_all(outgoing, 'fix', split_axis=0, concat_axis=0, tiled=True)  7.37 us
  transfers between devices with their start and end apart: 2, of which 2 were waited for; matrix products, arithmetic and copies ran while one was open for 26% of the time, Pallas kernels for 0%

commit v1 on v0

--- a/solution.py
+++ b/solution.py
@@ -41,7 +41,9 @@
         "bkij,bkjs->bis", conn_tiles, needed, precision=lax.Precision.HIGHEST
     ).reshape(block_count * block_size, subj_count)
     fitted_part = jnp.einsum("ns,fs->nf", nuisance_pinv, smoothed, precision=lax.Precision.HIGHEST)
-    fitted = lax.psum(fitted_part, "subj")
+    fitted = fitted_part
+    for hop in (1, 2, 4):
+        fitted = fitted + lax.ppermute(fitted, "subj", [(dev, dev ^ hop) for dev in range(8)])
     residual = smoothed - jnp.einsum("nf,ns->fs", fitted, nuisance, precision=lax.Precision.HIGHEST)
     partial_value = jnp.einsum("cs,fs->cf", design, residual, precision=lax.Precision.HIGHEST)
     return lax.psum_scatter(partial_value, "subj", scatter_dimension=0, tiled=True)

time: 233 us -> 283 us (1.21)
  waiting for transfers between devices: 74.4 us -> 141 us
  blocking collectives: 51.9 us -> 21.5 us
  starting transfers between devices: 7.41 us -> 21.2 us
    all_to_all x1, waiting for transfers between devices: 35.7 us -> 96 us  [per_device(): lax.all_to_all(outgoing, 'fix', split_axis=0, concat_axis=0, tiled=True)]
    psum x1 -> x0, blocking collectives: 30.4 us -> none  [per_device(): fitted = lax.psum(fitted_part, 'subj')]
    ppermute x0 -> x3, starting transfers between devices: none -> 13.9 us  [per_device(): lax.ppermute(fitted, 'subj', [(dev, dev ^ hop) for dev in range(8)])]
    ppermute x0 -> x3, waiting for transfers between devices: none -> 5.6 us  [per_device(): lax.ppermute(fitted, 'subj', [(dev, dev ^ hop) for dev in range(8)])]
  transfers between devices with their start and end apart: 2 -> 5, of which waited for: 2 -> 4; matrix products, arithmetic and copies ran while one was open for 26% -> 21% of each run, Pallas kernels for 0% -> 0%
where the time goes in v1:
time: 283 us; the launch traced here: 282 us
  waiting for transfers between devices  141 us (50%)
  local copies, waits for them, and re-layouts  70.1 us (25%)
  blocking collectives  21.5 us (8%)
  starting transfers between devices  21.2 us (7%)
  between operations  13.6 us (5%)
  matrix products  8.81 us (3%)
  other arithmetic  6.12 us (2%)
    all_to_all x1, waiting for transfers between devices, per_device(): lax.all_to_all(outgoing, 'fix', split_axis=0, concat_axis=0, tiled=True)  96 us
    gather x2, local copies, waits for them, and re-layouts, design_rows(): picked = jnp.take(contrast, perm_table, axis=1)  59.9 us
    reduce_scatter x1, waiting for transfers between devices, per_device(): lax.psum_scatter(partial_value, 'subj', scatter_dimension=0, tiled=True)  39.3 us
    all_to_all x1, blocking collectives, per_device(): lax.all_to_all(request.reshape(fix_count, capacity), 'fix', split_axis=0,...  21.5 us
    ppermute x3, starting transfers between devices, per_device(): lax.ppermute(fitted, 'subj', [(dev, dev ^ hop) for dev in range(8)])  13.9 us
    all_to_all x1, starting transfers between devices, per_device(): lax.all_to_all(outgoing, 'fix', split_axis=0, concat_axis=0, tiled=True)  7.23 us
  transfers between devices with their start and end apart: 5, of which 4 were waited for; matrix products, arithmetic and copies ran while one was open for 21% of the time, Pallas kernels for 0%

profile of v1, /device:TPU:6, one launch (start us, length us, event | category | flops | bytes accessed | tf_op | source)
XLA Modules:
  0.0 282.2 jit_solution(9617141045570340068)
XLA Ops:
  6.5 0.9 copy.43
  7.4 0.1 reshape.202
  7.5 0.1 reshape.203
  7.6 0.2 convert_reduce_fusion
  7.8 0.7 scatter_custom_fusion
  8.5 0.1 copy.49
  8.6 21.5 %all_to_all.20 = s32[64,1,1]{2,1,0:T(1,128)S(1)} all-to-all(s32[64,1,1]{2,1,0:T(1,128)S(1)} %copy.49), channel_id=1, replica_groups=mesh['fix'=64,'subj'=8] {'fix'}, dimensions={0} | all-to-all | bytes 512 | tf_op jit(solution)/shard_map/all_to_all | solution.py:28
  30.1 1.2 reduce
  31.4 3.8 %gather_fusion.1 = f32[64,128,128]{2,1,0:T(8,128)} fusion(f32[8,128,128]{2,1,0:T(8,128)} %bitcast.36, s32[1024]{0:T(1024)S(1)} %pad_clamp_fusion.1), kind=kCustom, calls=%fused_computation.1 | custom fusion | bytes 8388864 | tf_op jit(solution)/shard_map/jit(_take)/gather | solution.py:33
  35.2 4.5 %bitcast_select_fusion = f32[64,1,128,128]{3,2,1,0:T(8,128)} fusion(f32[64,128,128]{2,1,0:T(8,128)} %gather_fusion.1, pred[64]{0:T(512)(128)(4,1)S(1)} %compare_and_fusion.2), kind=kLoop, calls=%fused_computation.4 | loop fusion | flops 1048576 | bytes 8388672 | tf_op jit(solution)/shard_map/jit(_take)/select_n | solution.py:33
  39.7 7.2 %all-to-all-start.1 = ((f32[64,1,128,128]{3,2,1,0:T(8,128)}), f32[64,1,128,128]{3,2,1,0:T(8,128)}, u32[]{:S(2)}, u32[]{:S(2)}) async-start(f32[64,1,128,128]{3,2,1,0:T(8,128)} %bitcast_select_fusion), calls=%async_computation.1 | async-start | bytes 8388608 | tf_op jit(solution)/shard_map/all_to_all | solution.py:36
  46.9 0.0 reduce-scatter.2.cloned.1.call-start
  47.0 0.1 reduce_sum.14
  47.1 96.0 %all-to-all-done.1 = f32[64,1,128,128]{3,2,1,0:T(8,128)} async-done(((f32[64,1,128,128]{3,2,1,0:T(8,128)}), f32[64,1,128,128]{3,2,1,0:T(8,128)}, u32[]{:S(2)}, u32[]{:S(2)}) %all-to-all-start.1) | async-done | bytes 4194336 | tf_op jit(solution)/shard_map/all_to_all | solution.py:36
  143.1 4.2 %gather_fusion.2 = f32[32,128,128]{2,1,0:T(8,128)} fusion(f32[64,128,128]{2,1,0:T(8,128)} %bitcast.10, s32[1024]{0:T(1024)S(1)} %pad_clamp_fusion), kind=kCustom, calls=%fused_computation.2 | custom fusion | bytes 4194432 | tf_op jit(solution)/shard_map/jit(_take)/gather | solution.py:39
  147.3 4.1 %fusion = f32[8,128,128,1]{1,2,3,0:T(8,128)S(1)} fusion(f32[8,4,128,128]{3,2,1,0:T(8,128)S(1)} %copy-done, f32[8,4,128,128]{3,2,1,0:T(8,128)} %bitcast.38, pred[8,4]{1,0:T(8,128)(4,1)S(1)} %compare_and_fusion.1), kind=kOutput, calls=%fused_computation.5 | convolution fusion | flops 805830656 | bytes 4718624 | tf_op jit(solution)/shard_map/bkij,bkjs->bis/dot_general | solution.py:40
  151.5 0.5 convolution_bitcast_fusion
  152.0 3.5 %collective-permute-start = (f32[4,1024]{1,0:T(4,128)S(1)}, f32[4,1024]{1,0:T(4,128)S(1)}, u32[]{:S(2)}, u32[]{:S(2)}) collective-permute-start(f32[4,1024]{1,0:T(4,128)S(1)} %convolution_bitcast_fusion), channel_id=1, source_target_pairs={{0,1},{1,0},{2,3},{3,2},{4,5},{5,4},{6,7},{7,6},{8,9},{9,8},{10,11... | collective-permute-start | bytes 49160 | tf_op jit(solution)/shard_map/ppermute | solution.py:46
  155.5 0.0 copy-done.1
  155.5 2.1 collective-permute-done
  157.7 4.5 %collective-permute-start.1 = (f32[4,1024]{1,0:T(4,128)S(1)}, f32[4,1024]{1,0:T(4,128)S(1)}, u32[]{:S(2)}, u32[]{:S(2)}) collective-permute-start(f32[4,1024]{1,0:T(4,128)S(1)} %add.116), channel_id=1, source_target_pairs={{0,2},{1,3},{2,0},{3,1},{4,6},{5,7},{6,4},{7,5},{8,10},{9,11},{10,... | collective-permute-start | bytes 49160 | tf_op jit(solution)/shard_map/ppermute | solution.py:46
  162.2 0.2 copy.41
  162.4 54.4 %gather_fusion = f32[16384,4]{1,0:T(8,128)} fusion(f32[4,1024]{0,1:T(8,128)S(1)} %copy.41, s32[16384]{0:T(1024)S(1)} %bitcast_clamp_fusion), kind=kCustom, calls=%fused_computation | custom fusion | bytes 589824 | tf_op jit(solution)/shard_map/jit(_take)/gather | solution.py:8
  216.8 5.5 %copy.42 = f32[128,128,4]{1,2,0:T(4,128)S(1)} copy(f32[128,128,4]{2,1,0:T(8,128)} %bitcast.37) | data formatting | bytes 524288 | tf_op jit(solution)/shard_map/jit(_take)/gather | solution.py:8
  222.3 0.0 collective-permute-done.1
  222.3 5.9 %collective-permute-start.2 = (f32[4,1024]{1,0:T(4,128)S(1)}, f32[4,1024]{1,0:T(4,128)S(1)}, u32[]{:S(2)}, u32[]{:S(2)}) collective-permute-start(f32[4,1024]{1,0:T(4,128)S(1)} %add.117), channel_id=1, source_target_pairs={{0,4},{1,5},{2,6},{3,7},{4,0},{5,1},{6,2},{7,3},{8,12},{9,13},{10,... | collective-permute-start | bytes 49160 | tf_op jit(solution)/shard_map/ppermute | solution.py:46
  228.3 0.1 broadcast_select_fusion
  228.4 3.5 %collective-permute-done.2 = f32[4,1024]{1,0:T(4,128)S(1)} collective-permute-done((f32[4,1024]{1,0:T(4,128)S(1)}, f32[4,1024]{1,0:T(4,128)S(1)}, u32[]{:S(2)}, u32[]{:S(2)}) %collective-permute-start.2) | collective-permute-done | bytes 16416 | tf_op jit(solution)/shard_map/ppermute | solution.py:46
  231.9 1.0 convolution_subtract_fusion
  232.9 3.1 %fusion.14 = f32[512,1024]{1,0:T(8,128)} fusion(f32[512,128]{1,0:T(8,128)S(1)} %bitcast.41, f32[1024,128]{1,0:T(8,128)S(1)} %convolution_subtract_fusion), kind=kOutput, calls=%fused_computation.50 | convolution fusion | flops 805306368 | bytes 2883584 | tf_op jit(solution)/shard_map/cs,fs->cf/dot_general | solution.py:48
  236.0 0.0 reduce-scatter.2.cloned.1.call-update
  236.1 39.3 %reduce-scatter.2.cloned.1.call-done = f32[64,1024]{1,0:T(8,128)} async-done(((f32[512,1024]{1,0:T(8,128)}), f32[64,1024]{1,0:T(8,128)}) %reduce-scatter.2.cloned.1.call-update) | async-done | bytes 262160 | tf_op jit(solution)/shard_map/reduce_scatter | solution.py:49
  (20 shorter events, 0.1 us)
Async XLA Ops:
  6.5 140.8 %copy-start = (f32[8,4,128,128]{3,2,1,0:T(8,128)S(1)}, f32[8,4,128,128]{3,2,1,0:T(8,128)}, u32[]{:S(2)}) copy-start(f32[8,4,128,128]{3,2,1,0:T(8,128)} %param.8) | copy-start | bytes 6291460
  39.7 103.4 %all-to-all-start.1 = ((f32[64,1,128,128]{3,2,1,0:T(8,128)}), f32[64,1,128,128]{3,2,1,0:T(8,128)}, u32[]{:S(2)}, u32[]{:S(2)}) async-start(f32[64,1,128,128]{3,2,1,0:T(8,128)} %bitcast_select_fusion), calls=%async_computation.1 | async-start | bytes 8388608 | tf_op jit(solution)/shard_map/all_to_all | solution.py:36
  46.9 228.5 %reduce-scatter.2.cloned.1.call-start = ((), (), s32[]{:S(2)}) async-start(), calls=%async_computation.3 | async-start | bytes 2359296 | tf_op jit(solution)/shard_map/reduce_scatter | solution.py:49
  147.3 4.1 %copy-start.3 = (f32[4,128]{1,0:T(4,128)S(1)}, f32[4,128]{1,0:T(4,128)}, u32[]{:S(2)}) copy-start(f32[4,128]{1,0:T(4,128)} %param.11) | copy-start | bytes 6148
  147.3 8.2 %copy-start.1 = (s32[128,128]{1,0:T(8,128)S(1)}, s32[128,128]{1,0:T(8,128)}, u32[]{:S(2)}) copy-start(s32[128,128]{1,0:T(8,128)} %param.13) | copy-start | bytes 196612
  147.3 14.9 %copy-start.2 = (f32[4,1024]{1,0:T(4,128)S(1)}, f32[4,1024]{1,0:T(4,128)}, u32[]{:S(2)}) copy-start(f32[4,1024]{1,0:T(4,128)} %param.12) | copy-start | bytes 49156
  152.0 5.6 %collective-permute-start = (f32[4,1024]{1,0:T(4,128)S(1)}, f32[4,1024]{1,0:T(4,128)S(1)}, u32[]{:S(2)}, u32[]{:S(2)}) collective-permute-start(f32[4,1024]{1,0:T(4,128)S(1)} %convolution_bitcast_fusion), channel_id=1, source_target_pairs={{0,1},{1,0},{2,3},{3,2},{4,5},{5,4},{6,7},{7,6},{8,9},{9,8},{10,11... | collective-permute-start | bytes 49160 | tf_op jit(solution)/shard_map/ppermute | solution.py:46
  157.7 64.7 %collective-permute-start.1 = (f32[4,1024]{1,0:T(4,128)S(1)}, f32[4,1024]{1,0:T(4,128)S(1)}, u32[]{:S(2)}, u32[]{:S(2)}) collective-permute-start(f32[4,1024]{1,0:T(4,128)S(1)} %add.116), channel_id=1, source_target_pairs={{0,2},{1,3},{2,0},{3,1},{4,6},{5,7},{6,4},{7,5},{8,10},{9,11},{10,... | collective-permute-start | bytes 49160 | tf_op jit(solution)/shard_map/ppermute | solution.py:46
  216.8 15.1 %copy-start.4 = (f32[4,128]{1,0:T(4,128)S(1)}, f32[4,128]{1,0:T(4,128)}, u32[]{:S(2)}) copy-start(f32[4,128]{1,0:T(4,128)} %param.10) | copy-start | bytes 6148
  222.3 9.5 %collective-permute-start.2 = (f32[4,1024]{1,0:T(4,128)S(1)}, f32[4,1024]{1,0:T(4,128)S(1)}, u32[]{:S(2)}, u32[]{:S(2)}) collective-permute-start(f32[4,1024]{1,0:T(4,128)S(1)} %add.117), channel_id=1, source_target_pairs={{0,4},{1,5},{2,6},{3,7},{4,0},{5,1},{6,2},{7,3},{8,12},{9,13},{10,... | collective-permute-start | bytes 49160 | tf_op jit(solution)/shard_map/ppermute | solution.py:46
Sparse Core Ops, SparseCore 0:
  236.2 39.1 reduce-scatter.1
